TPU v7x, 32 devices: a whole 2x2x4 slice. The times are simulated.
32 devices in a mesh: seq: 4 (over y, x), ctx: 8 (over z, core).
Axes of the slice: x: 2, y: 2, z: 4, core: 2. Of those that a mesh axis runs over, the one named last changes fastest.
Arguments:
- inputs: bfloat16 [4096, 1152], P(('seq', 'ctx')), may hold values from -140 to 140
- positions: int32 [4096], P(('seq', 'ctx')), may hold values from 0 to 1023, as said below
- attention_gain: bfloat16 [1152], P(('seq', 'ctx')), may hold values from 0.3984375 to 1.59375
- query_weight: bfloat16 [1152, 1024], P(('seq', 'ctx')), may hold values from -0.1875 to 0.1875
- key_weight: bfloat16 [1152, 256], P(('seq', 'ctx')), may hold values from -0.1875 to 0.1875
- value_weight: bfloat16 [1152, 256], P(('seq', 'ctx')), may hold values from -0.1875 to 0.1875
- query_gain: bfloat16 [256], P(('seq', 'ctx')), may hold values from 0.5 to 1.5
- key_gain: bfloat16 [256], P(('seq', 'ctx')), may hold values from 0.5 to 1.5
- output_weight: bfloat16 [1024, 1152], P(('seq', 'ctx')), may hold values from -0.1875 to 0.1875
- attention_post: bfloat16 [1152], P(('seq', 'ctx')), may hold values from 0.3984375 to 1.59375
- feedfwd_gain: bfloat16 [1152], P(('seq', 'ctx')), may hold values from 0.3984375 to 1.59375
- gate_weight: bfloat16 [1152, 6912], P(('seq', 'ctx')), may hold values from -0.1875 to 0.1875
- up_weight: bfloat16 [1152, 6912], P(('seq', 'ctx')), may hold values from -0.1875 to 0.1875
- down_weight: bfloat16 [6912, 1152], P(('seq', 'ctx')), may hold values from -0.078125 to 0.078125
- feedfwd_post: bfloat16 [1152], P(('seq', 'ctx')), may hold values from 0.3984375 to 1.59375
- cotangent: bfloat16 [4096, 1152], P(('seq', 'ctx')), may hold values from -6 to 6
Outputs:
- block_out: bfloat16 [4096, 1152], P(('seq', 'ctx'))
- input_grad: float32 [4096, 1152], P(('seq', 'ctx'))
- attention_gain_grad: float32 [1152], P(('seq', 'ctx'))
- query_grad: float32 [1152, 1024], P(('seq', 'ctx'))
- key_grad: float32 [1152, 256], P(('seq', 'ctx'))
- value_grad: float32 [1152, 256], P(('seq', 'ctx'))
- query_gain_grad: float32 [256], P(('seq', 'ctx'))
- key_gain_grad: float32 [256], P(('seq', 'ctx'))
- output_grad: float32 [1024, 1152], P(('seq', 'ctx'))
- attention_post_grad: float32 [1152], P(('seq', 'ctx'))
- feedfwd_gain_grad: float32 [1152], P(('seq', 'ctx'))
- gate_grad: float32 [1152, 6912], P(('seq', 'ctx'))
- up_grad: float32 [1152, 6912], P(('seq', 'ctx'))
- down_grad: float32 [6912, 1152], P(('seq', 'ctx'))
- feedfwd_post_grad: float32 [1152], P(('seq', 'ctx'))
Inputs may be any that keep to these rules, and one draw needn't show every extreme that they name: Within each sequence of 1024 tokens, the 128 tokens of each ctx index hold the consecutive positions k * 128 to k * 128 + 127, where the block numbers k of one sequence's ctx indices are a permutation of 0 to 7, drawn afresh for every sequence.
All inputs are finite; a program needn't handle non-finite values.
Results may differ from a plain program's by a relative error of at most 0.038.
Values may be sent and summed in bfloat16 or wider, within the bound.
A program may use at most 448 MiB of HBM per device.

v0:
```python
import math
import jax
import jax.numpy as jnp
from jax import lax
from jax.sharding import PartitionSpec as P

D = 1152
H = 4
DH = 256
FF = 6912
EPSILON = 1e-06
THETA = 1000000.0
GELU_COEF = math.sqrt(2.0 / math.pi)


def rms_factor(values):
    return lax.rsqrt(jnp.mean(values * values, axis=-1, keepdims=True) + EPSILON)


def norm_back(values, factor, gain_vector, upstream):
    scaled = gain_vector * upstream
    cubed = factor * factor * factor
    return factor * scaled - values * cubed * jnp.mean(scaled * values, axis=-1, keepdims=True)


def rotary(places):
    half_width = DH // 2
    exponent = jnp.arange(half_width, dtype=jnp.float32) * (-2.0 / DH)
    frequency = jnp.power(jnp.float32(THETA), exponent)
    angles = places.astype(jnp.float32)[:, None] * frequency[None, :]
    return (jnp.cos(angles), jnp.sin(angles))


def rotate(values, cosine, sinus):
    half_width = values.shape[-1] // 2
    first = values[..., :half_width]
    second = values[..., half_width:]
    return jnp.concatenate(
        [first * cosine - second * sinus, second * cosine + first * sinus], axis=-1
    )


def rotate_back(upstream, cosine, sinus):
    half_width = upstream.shape[-1] // 2
    first = upstream[..., :half_width]
    second = upstream[..., half_width:]
    return jnp.concatenate(
        [first * cosine + second * sinus, second * cosine - first * sinus], axis=-1
    )


def gelu_tanh(values):
    inner = GELU_COEF * (values + 0.044715 * values * values * values)
    return 0.5 * values * (1.0 + jnp.tanh(inner))


def gelu_slope(values):
    inner = GELU_COEF * (values + 0.044715 * values * values * values)
    tangent = jnp.tanh(inner)
    return 0.5 * (1.0 + tangent) + 0.5 * values * (1.0 - tangent * tangent) * GELU_COEF * (
        1.0 + 3.0 * 0.044715 * values * values
    )


def times_right(left_side, right_side):
    return jnp.dot(left_side, right_side, preferred_element_type=jnp.float32)


def times_transposed(left_side, right_side):
    return lax.dot_general(
        left_side, right_side, (((1,), (1,)), ((), ())), preferred_element_type=jnp.float32
    )


def transposed_times(left_side, right_side):
    return lax.dot_general(
        left_side, right_side, (((0,), (0,)), ((), ())), preferred_element_type=jnp.float32
    )


def attend_back(
    query_part, place_part, output_part, logsum_part, upper_part, key_all, value_all, place_all
):
    scaling = 1.0 / math.sqrt(DH)
    upper_round = upper_part.astype(jnp.bfloat16)
    row_delta = jnp.sum(upper_part * output_part.astype(jnp.float32), axis=-1)
    scores = (
        jnp.einsum("qhd,kd->hqk", query_part, key_all, preferred_element_type=jnp.float32) * scaling
    )
    allowed = place_all[None, None, :] <= place_part[None, :, None]
    probability = jnp.where(allowed, jnp.exp(scores - jnp.transpose(logsum_part)[:, :, None]), 0.0)
    value_sum = jnp.einsum(
        "hqk,qhd->kd",
        probability.astype(jnp.bfloat16),
        upper_round,
        preferred_element_type=jnp.float32,
    )
    prob_back = jnp.einsum(
        "qhd,kd->hqk", upper_round, value_all, preferred_element_type=jnp.float32
    )
    score_back = (
        probability * (prob_back - jnp.transpose(row_delta)[:, :, None]) * scaling
    ).astype(jnp.bfloat16)
    query_back = jnp.einsum("hqk,kd->qhd", score_back, key_all, preferred_element_type=jnp.float32)
    key_back = jnp.einsum("hqk,qhd->kd", score_back, query_part, preferred_element_type=jnp.float32)
    return (query_back, key_back, value_sum)


def per_device(
    inputs,
    positions,
    attention_gain,
    query_weight,
    key_weight,
    value_weight,
    query_gain,
    key_gain,
    output_weight,
    attention_post,
    feedfwd_gain,
    gate_weight,
    up_weight,
    down_weight,
    feedfwd_post,
    cotangent,
):
    attention_set = (
        lax.all_gather(attention_gain, ("seq", "ctx"), axis=0, tiled=True),
        lax.all_gather(query_weight, ("seq", "ctx"), axis=0, tiled=True),
        lax.all_gather(key_weight, ("seq", "ctx"), axis=0, tiled=True),
        lax.all_gather(value_weight, ("seq", "ctx"), axis=0, tiled=True),
        lax.all_gather(query_gain, ("seq", "ctx"), axis=0, tiled=True),
        lax.all_gather(key_gain, ("seq", "ctx"), axis=0, tiled=True),
        lax.all_gather(output_weight, ("seq", "ctx"), axis=0, tiled=True),
        lax.all_gather(attention_post, ("seq", "ctx"), axis=0, tiled=True),
    )
    feedfwd_set = (
        lax.all_gather(feedfwd_gain, ("seq", "ctx"), axis=0, tiled=True),
        lax.all_gather(gate_weight, ("seq", "ctx"), axis=0, tiled=True),
        lax.all_gather(up_weight, ("seq", "ctx"), axis=0, tiled=True),
        lax.all_gather(down_weight, ("seq", "ctx"), axis=0, tiled=True),
        lax.all_gather(feedfwd_post, ("seq", "ctx"), axis=0, tiled=True),
    )
    gain_attention = attention_set[0].astype(jnp.float32)
    gain_query = attention_set[4].astype(jnp.float32)
    gain_key = attention_set[5].astype(jnp.float32)
    gain_post = attention_set[7].astype(jnp.float32)
    gain_feed = feedfwd_set[0].astype(jnp.float32)
    gain_final = feedfwd_set[4].astype(jnp.float32)
    token_count = inputs.shape[0]
    scaling = 1.0 / math.sqrt(DH)
    device_total = lax.axis_size(("seq", "ctx"))
    input_wide = inputs.astype(jnp.float32)
    input_factor = rms_factor(input_wide)
    normed = (input_wide * input_factor * gain_attention).astype(jnp.bfloat16)
    queries = times_right(normed, attention_set[1]).reshape(token_count, H, DH)
    key_rows = times_right(normed, attention_set[2])
    value_rows = times_right(normed, attention_set[3]).astype(jnp.bfloat16)
    cosine, sinus = rotary(positions)
    query_factor = rms_factor(queries)
    query_rot = rotate(
        queries * query_factor * gain_query, cosine[:, None, :], sinus[:, None, :]
    ).astype(jnp.bfloat16)
    key_factor = rms_factor(key_rows)
    key_rot = rotate(key_rows * key_factor * gain_key, cosine, sinus).astype(jnp.bfloat16)
    key_piece = lax.all_gather(key_rot, "ctx", axis=0, tiled=True)
    value_piece = lax.all_gather(value_rows, "ctx", axis=0, tiled=True)
    place_piece = lax.all_gather(positions, "ctx", axis=0, tiled=True)
    scores = (
        jnp.einsum("qhd,kd->hqk", query_rot, key_piece, preferred_element_type=jnp.float32)
        * scaling
    )
    allowed = place_piece[None, None, :] <= positions[None, :, None]
    expscore = jnp.where(allowed, jnp.exp(scores), 0.0)
    weight_sum = jnp.sum(expscore, axis=-1)
    summed = jnp.einsum(
        "hqk,kd->qhd",
        expscore.astype(jnp.bfloat16),
        value_piece,
        preferred_element_type=jnp.float32,
    )
    weight_sum, summed = (weight_sum, summed)
    attended_heads = (summed / jnp.transpose(weight_sum)[:, :, None]).astype(jnp.bfloat16)
    logsum = jnp.transpose(jnp.log(weight_sum))
    attended = attended_heads.reshape(token_count, H * DH)
    mixed_values = times_right(attended, attention_set[6])
    mixed_factor = rms_factor(mixed_values)
    residual = input_wide + mixed_values * mixed_factor * gain_post
    residual_factor = rms_factor(residual)
    fed_rows = (residual * residual_factor * gain_feed).astype(jnp.bfloat16)
    gate_values = times_right(fed_rows, feedfwd_set[1])
    up_values = times_right(fed_rows, feedfwd_set[2])
    hidden = (gelu_tanh(gate_values) * up_values).astype(jnp.bfloat16)
    down_values = times_right(hidden, feedfwd_set[3])
    down_factor = rms_factor(down_values)
    block_out = (residual + down_values * down_factor * gain_final).astype(jnp.bfloat16)
    feedfwd_back = (
        lax.all_gather(feedfwd_gain, ("seq", "ctx"), axis=0, tiled=True),
        lax.all_gather(gate_weight, ("seq", "ctx"), axis=0, tiled=True),
        lax.all_gather(up_weight, ("seq", "ctx"), axis=0, tiled=True),
        lax.all_gather(down_weight, ("seq", "ctx"), axis=0, tiled=True),
        lax.all_gather(feedfwd_post, ("seq", "ctx"), axis=0, tiled=True),
    )
    cot_wide = cotangent.astype(jnp.float32)
    grad_final = jnp.sum(cot_wide * down_values * down_factor, axis=0)
    down_back = norm_back(down_values, down_factor, gain_final, cot_wide).astype(jnp.bfloat16)
    hidden_back = times_transposed(down_back, feedfwd_back[3])
    gate_back = (hidden_back * up_values * gelu_slope(gate_values)).astype(jnp.bfloat16)
    up_back = (hidden_back * gelu_tanh(gate_values)).astype(jnp.bfloat16)
    fed_back = times_transposed(gate_back, feedfwd_back[1]) + times_transposed(
        up_back, feedfwd_back[2]
    )
    grad_feed = jnp.sum(fed_back * residual * residual_factor, axis=0)
    residual_back = cot_wide + norm_back(residual, residual_factor, gain_feed, fed_back)
    grad_post = jnp.sum(residual_back * mixed_values * mixed_factor, axis=0)
    mixed_back = norm_back(mixed_values, mixed_factor, gain_post, residual_back).astype(
        jnp.bfloat16
    )
    out_share = H * DH // device_total
    down_share = FF // device_total
    column_share = out_share + down_share
    shard_count = column_share * lax.axis_size(("seq", "ctx")) // column_share
    out_term = transposed_times(attended, mixed_back).reshape(shard_count, out_share, D)
    down_term = transposed_times(hidden, down_back).reshape(shard_count, down_share, D)
    column_block = lax.psum_scatter(
        jnp.concatenate([out_term, down_term], axis=1).reshape(
            column_share * lax.axis_size(("seq", "ctx")), D
        ),
        ("seq", "ctx"),
        scatter_dimension=0,
        tiled=True,
    )
    grad_output = column_block[:out_share]
    grad_down = column_block[out_share:]
    attention_back = (
        lax.all_gather(attention_gain, ("seq", "ctx"), axis=0, tiled=True),
        lax.all_gather(query_weight, ("seq", "ctx"), axis=0, tiled=True),
        lax.all_gather(key_weight, ("seq", "ctx"), axis=0, tiled=True),
        lax.all_gather(value_weight, ("seq", "ctx"), axis=0, tiled=True),
        lax.all_gather(query_gain, ("seq", "ctx"), axis=0, tiled=True),
        lax.all_gather(key_gain, ("seq", "ctx"), axis=0, tiled=True),
        lax.all_gather(output_weight, ("seq", "ctx"), axis=0, tiled=True),
        lax.all_gather(attention_post, ("seq", "ctx"), axis=0, tiled=True),
    )
    attended_back = times_transposed(mixed_back, attention_back[6]).reshape(token_count, H, DH)
    key_all, value_all, place_all = (
        lax.all_gather(key_rot, "ctx", axis=0, tiled=True),
        lax.all_gather(value_rows, "ctx", axis=0, tiled=True),
        lax.all_gather(positions, "ctx", axis=0, tiled=True),
    )
    block_len = min(token_count, 128)
    block_count = token_count // block_len

    def back_block(state_now, pieces):
        query_part, place_part, output_part, logsum_part, upper_part = pieces
        query_back, key_back, value_sum = attend_back(
            query_part,
            place_part,
            output_part,
            logsum_part,
            upper_part,
            key_all,
            value_all,
            place_all,
        )
        return ((state_now[0] + key_back, state_now[1] + value_sum), query_back)

    zero_rows = jnp.zeros((key_all.shape[0], DH), jnp.float32)
    blocks_in = (
        query_rot.reshape(block_count, block_len, H, DH),
        positions.reshape(block_count, block_len),
        attended_heads.reshape(block_count, block_len, H, DH),
        logsum.reshape(block_count, block_len, H),
        attended_back.reshape(block_count, block_len, H, DH),
    )
    (key_terms, value_terms), query_parts = lax.scan(back_block, (zero_rows, zero_rows), blocks_in)
    own_rows = lax.psum_scatter(
        jnp.concatenate([key_terms, value_terms], axis=1).astype(jnp.bfloat16),
        "ctx",
        scatter_dimension=0,
        tiled=True,
    ).astype(jnp.float32)
    key_rot_back = own_rows[:, :DH]
    value_back = own_rows[:, DH:].astype(jnp.bfloat16)
    query_rot_back = query_parts.reshape(token_count, H, DH)
    query_up = rotate_back(query_rot_back, cosine[:, None, :], sinus[:, None, :])
    grad_qgain = jnp.sum(query_up * queries * query_factor, axis=(0, 1))
    query_back = (
        norm_back(queries, query_factor, gain_query, query_up)
        .astype(jnp.bfloat16)
        .reshape(token_count, H * DH)
    )
    key_up = rotate_back(key_rot_back, cosine, sinus)
    grad_kgain = jnp.sum(key_up * key_rows * key_factor, axis=0)
    key_back = norm_back(key_rows, key_factor, gain_key, key_up).astype(jnp.bfloat16)
    normed_back = (
        times_transposed(query_back, attention_back[1])
        + times_transposed(key_back, attention_back[2])
        + times_transposed(value_back, attention_back[3])
    )
    grad_attention = jnp.sum(normed_back * input_wide * input_factor, axis=0)
    input_grad = residual_back + norm_back(input_wide, input_factor, gain_attention, normed_back)
    attention_backs = jnp.concatenate([query_back, key_back, value_back], axis=1)
    feedfwd_backs = jnp.concatenate([gate_back, up_back], axis=1)
    row_block = lax.psum_scatter(
        jnp.concatenate(
            [transposed_times(normed, attention_backs), transposed_times(fed_rows, feedfwd_backs)],
            axis=1,
        ),
        ("seq", "ctx"),
        scatter_dimension=0,
        tiled=True,
    )
    grad_query = row_block[:, : H * DH]
    grad_key = row_block[:, H * DH : H * DH + DH]
    grad_value = row_block[:, H * DH + DH : H * DH + 2 * DH]
    grad_gate = row_block[:, H * DH + 2 * DH : H * DH + 2 * DH + FF]
    grad_up = row_block[:, H * DH + 2 * DH + FF :]
    gains_summed = (
        lax.psum_scatter(grad_attention, ("seq", "ctx"), scatter_dimension=0, tiled=True),
        lax.psum_scatter(grad_qgain, ("seq", "ctx"), scatter_dimension=0, tiled=True),
        lax.psum_scatter(grad_kgain, ("seq", "ctx"), scatter_dimension=0, tiled=True),
        lax.psum_scatter(grad_post, ("seq", "ctx"), scatter_dimension=0, tiled=True),
        lax.psum_scatter(grad_feed, ("seq", "ctx"), scatter_dimension=0, tiled=True),
        lax.psum_scatter(grad_final, ("seq", "ctx"), scatter_dimension=0, tiled=True),
    )
    return (
        block_out,
        input_grad,
        gains_summed[0],
        grad_query,
        grad_key,
        grad_value,
        gains_summed[1],
        gains_summed[2],
        grad_output,
        gains_summed[3],
        gains_summed[4],
        grad_gate,
        grad_up,
        grad_down,
        gains_summed[5],
    )


def solution(mesh):
    return jax.shard_map(
        per_device,
        mesh=mesh,
        in_specs=(
            P(("seq", "ctx"), None),
            P(("seq", "ctx")),
            P(("seq", "ctx")),
            P(("seq", "ctx"), None),
            P(("seq", "ctx"), None),
            P(("seq", "ctx"), None),
            P(("seq", "ctx")),
            P(("seq", "ctx")),
            P(("seq", "ctx"), None),
            P(("seq", "ctx")),
            P(("seq", "ctx")),
            P(("seq", "ctx"), None),
            P(("seq", "ctx"), None),
            P(("seq", "ctx"), None),
            P(("seq", "ctx")),
            P(("seq", "ctx"), None),
        ),
        out_specs=(
            P(("seq", "ctx"), None),
            P(("seq", "ctx"), None),
            P(("seq", "ctx")),
            P(("seq", "ctx"), None),
            P(("seq", "ctx"), None),
            P(("seq", "ctx"), None),
            P(("seq", "ctx")),
            P(("seq", "ctx")),
            P(("seq", "ctx"), None),
            P(("seq", "ctx")),
            P(("seq", "ctx")),
            P(("seq", "ctx"), None),
            P(("seq", "ctx"), None),
            P(("seq", "ctx"), None),
            P(("seq", "ctx")),
        ),
        check_vma=False,
    )
```

profile of v0, /device:TPU:0, one launch (start us, length us, event | category | flops | bytes accessed | tf_op | source)
XLA Modules:
  0.0 2184.4 jit_solution(18043881758278048469)
XLA Ops:
  16.4 42.4 %all-reduce.16 = (bf16[1152]{0:T(1024)(128)(2,1)S(1)}, bf16[256]{0:T(256)(128)(2,1)S(1)}, bf16[256]{0:T(256)(128)(2,1)S(1)}, bf16[1152]{0:T(1024)(128)(2,1)S(1)}...) all-reduce(bf16[1152]{0:T(1024)(128)(2,1)S(1)} %dynamic-update-slic, ...), channel_id=1, replica_groups=mesh['seq'=4,'ctx'=8] {'seq','ctx'}, use_global_device_ids=true, to_apply=%add | all-reduce | flops 5120 | bytes 20480
  60.6 43.6 %all-gather.2 = bf16[32,36,256]{2,1,0:T(8,128)(2,1)S(1)} all-gather(bf16[1,36,256]{2,1,0:T(8,128)(2,1)} %bitcast.148), channel_id=1, replica_groups=mesh['seq'=4,'ctx'=8] {'seq','ctx'}, dimensions={0}, use_global_device_ids=true | all-gather | bytes 608256 | tf_op jit(solution)/shard_map/all_gather | solution.py:130
  104.4 40.5 %all-gather = bf16[32,36,256]{2,1,0:T(8,128)(2,1)S(1)} all-gather(bf16[1,36,256]{2,1,0:T(8,128)(2,1)S(1)} %bitcast.149), channel_id=1, replica_groups=mesh['seq'=4,'ctx'=8] {'seq','ctx'}, dimensions={0}, use_global_device_ids=true | all-gather | bytes 608256 | tf_op jit(solution)/shard_map/all_gather | solution.py:131
  145.1 10.4 all-gather.1
  159.0 18.2 all_gather.64
  177.5 18.4 all_gather.60
  196.0 2.7 reshape.304
  206.8 2.4 multiply_reduce_fusion.6
  211.0 45.9 %all-gather.18.cloned.1.call-done = bf16[32,36,6912]{2,1,0:T(8,128)(2,1)} async-done(((bf16[1,36,6912]{2,1,0:T(8,128)(2,1)}), bf16[32,36,6912]{2,1,0:T(8,128)(2,1)}) %all-gather.18.cloned.1.call-update) | async-done | bytes 15925264 | tf_op jit(solution)/shard_map/all_gather | solution.py:139
  256.9 18.5 reshape.306
  275.3 101.3 %all-gather.20.cloned.1.call-done = bf16[32,36,6912]{2,1,0:T(8,128)(2,1)} async-done(((bf16[1,36,6912]{2,1,0:T(8,128)(2,1)}), bf16[32,36,6912]{2,1,0:T(8,128)(2,1)}) %all-gather.20.cloned.1.call-update) | async-done | bytes 15925264 | tf_op jit(solution)/shard_map/all_gather | solution.py:140
  376.6 18.9 reshape.308
  395.5 8.2 fusion.98
  403.8 1.8 copy-done.3
  406.9 4.6 multiply_convert_fusion.1
  411.6 76.7 %all-gather.14.cloned.1.call-done = bf16[6912,1152]{1,0:T(8,128)(2,1)} async-done(((bf16[216,1152]{1,0:T(8,128)(2,1)}), bf16[6912,1152]{1,0:T(8,128)(2,1)}) %all-gather.14.cloned.1.call-update) | async-done | bytes 15925264 | tf_op jit(solution)/shard_map/all_gather | solution.py:141
  488.3 8.2 multiply_reduce_fusion.4
  498.3 10.4 multiply_convert_fusion
  508.8 11.2 fusion.99
  520.0 12.6 multiply_reduce_fusion
  532.7 2.3 multiply_reduce_fusion.1
  540.2 12.6 fusion.101
  552.8 25.1 %fusion.7 = f32[1152,13824]{1,0:T(8,128)} fusion(bf16[128,1152]{1,0:T(8,128)(2,1)S(1)} %multiply_convert_fusion.2, bf16[128,6912]{1,0:T(8,128)(2,1)} %get-tuple-element.82, bf16[128,6912]{1,0:T(8,128)(2,1)} %copy-done.9), kind=kOutput, calls=%fused_computation.11 | convolution fusion | flops 4083941376 | bytes 67534848 | tf_op jit(solution)/shard_map/dot_general | solution.py:76
  581.0 24.9 %pad_maximum_fusion.1 = f32[32,248,1152]{2,1,0:T(8,128)} fusion(f32[32,216,1152]{2,1,0:T(8,128)} %bitcast.130, f32[32,32,1152]{2,1,0:T(8,128)S(1)} %fusion.63), kind=kLoop, calls=%fused_computation.1 | loop fusion | flops 9142272 | bytes 73138176 | tf_op jit(solution)/shard_map/concatenate | solution.py:226
  605.9 4.2 reduce-scatter.2.cloned.1.call-done
  612.5 4.0 fusion.57
  616.5 47.3 %pad_maximum_fusion = f32[1152,15360]{1,0:T(8,128)} fusion(f32[1152,13824]{1,0:T(8,128)} %fusion.7, f32[1152,1536]{1,0:T(8,128)} %fusion.57), kind=kLoop, calls=%fused_computation | loop fusion | flops 17694720 | bytes 141557760 | tf_op jit(solution)/shard_map/concatenate | solution.py:306
  669.5 40.2 %all-reduce.14 = (f32[1152]{0:T(1024)S(1)}, f32[256]{0:T(256)S(1)}, f32[256]{0:T(256)S(1)}, f32[1152]{0:T(1024)S(1)}, f32[1152]{0:T(1024)S(1)}, /*index=5*/f32[1152]{0:T(1024)S(1)}) all-reduce(f32[1152]{0:T(1024)S(1)} %get-tuple-element.57, f32[256]{0:T(256)S(1)} %reduce_sum.205, ...), channel_id=3, replica_groups=mesh['seq'=4,'ctx'=8] {'seq','ctx'}, use_global_device_ids=true, to_apply=%region_16.17.clone | all-reduce | flops 5120 | bytes 40960
  714.3 1452.1 %all-reduce.19.cloned.1.call-done = (f32[1152,15360]{1,0:T(8,128)}, f32[7936,1152]{1,0:T(8,128)}) async-done(((f32[1152,15360]{1,0:T(8,128)}, f32[7936,1152]{1,0:T(8,128)}), (f32[1152,15360]{1,0:T(8,128)}, f32[7936,1152]{1,0:T(8,128)})) %all-reduce.19.cloned.1.call-update) | async-done | bytes 107347984
  2168.0 2.2 constant_dynamic-slice_fusion.2
  2171.9 1.7 fusion.97
  2173.6 3.7 fusion.96
  (253 shorter events, 51.8 us)
Async XLA Ops:
  7.2 137.9 %copy-start.63 = (s32[128]{0:T(128)S(1)}, s32[128]{0:T(128)}, u32[]{:S(2)}) copy-start(s32[128]{0:T(128)} %param.17) | copy-start | bytes 1540
  7.2 97.2 %copy-start.45 = (bf16[36,256]{1,0:T(8,128)(2,1)S(1)}, bf16[36,256]{1,0:T(8,128)(2,1)}, u32[]{:S(2)}) copy-start(bf16[36,256]{1,0:T(8,128)(2,1)} %param.21) | copy-start | bytes 55300
  7.2 148.3 %copy-start.5 = (bf16[128,1152]{1,0:T(8,128)(2,1)S(1)}, bf16[128,1152]{1,0:T(8,128)(2,1)}, u32[]{:S(2)}) copy-start(bf16[128,1152]{1,0:T(8,128)(2,1)} %param.16) | copy-start | bytes 884740
  7.2 188.7 %all-gather.16.cloned.1.call-start = ((), (), s32[]{:S(2)}) async-start(), calls=%async_computation.4 | async-start | bytes 2703360 | tf_op jit(solution)/shard_map/all_gather | solution.py:129
  7.9 198.9 %all-gather.12.cloned.1.call-start = ((), (), s32[]{:S(2)}) async-start(), calls=%async_computation.1 | async-start | bytes 2433024 | tf_op jit(solution)/shard_map/all_gather | solution.py:134
  8.7 248.2 %all-gather.18.cloned.1.call-start = ((), (), s32[]{:S(2)}) async-start(), calls=%async_computation.5 | async-start | bytes 18247680 | tf_op jit(solution)/shard_map/all_gather | solution.py:139
  9.4 367.2 %all-gather.20.cloned.1.call-start = ((), (), s32[]{:S(2)}) async-start(), calls=%async_computation.6 | async-start | bytes 18247680 | tf_op jit(solution)/shard_map/all_gather | solution.py:140
  10.0 478.3 %all-gather.14.cloned.1.call-start = ((), (), s32[]{:S(2)}) async-start(), calls=%async_computation.2 | async-start | bytes 16422912 | tf_op jit(solution)/shard_map/all_gather | solution.py:141
  10.6 599.5 %reduce-scatter.2.cloned.1.call-start = ((), (), s32[]{:S(2)}) async-start(), calls=%async_computation.3 | async-start | bytes 1179648 | tf_op jit(solution)/shard_map/reduce_scatter | solution.py:277
  11.3 166.2 %copy-start.59 = (f32[128]{0:T(128)}, f32[128]{0:T(128)S(1)}, u32[]{:S(2)}) copy-start(f32[128]{0:T(128)S(1)} %convert_element_type.95) | copy-start | bytes 1540
  58.8 98.4 %copy-start.49 = (f32[256]{0:T(256)}, f32[256]{0:T(256)S(1)}, u32[]{:S(2)}) copy-start(f32[256]{0:T(256)S(1)} %convert_element_type.94) | copy-start | bytes 3076
  58.8 145.3 %copy-start.51 = (f32[256]{0:T(256)}, f32[256]{0:T(256)S(1)}, u32[]{:S(2)}) copy-start(f32[256]{0:T(256)S(1)} %convert_element_type.96) | copy-start | bytes 3076
  104.4 91.5 %copy-start.13 = (bf16[1152,256]{1,0:T(8,128)(2,1)}, bf16[1152,256]{1,0:T(8,128)(2,1)S(1)}, u32[]{:S(2)}) copy-start(bf16[1152,256]{1,0:T(8,128)(2,1)S(1)} %reshape.302) | copy-start | bytes 1769476
  145.0 50.9 %copy-start.14 = (bf16[1152,256]{1,0:T(8,128)(2,1)}, bf16[1152,256]{1,0:T(8,128)(2,1)S(1)}, u32[]{:S(2)}) copy-start(bf16[1152,256]{1,0:T(8,128)(2,1)S(1)} %reshape.298) | copy-start | bytes 1769476
  155.5 43.1 %copy-start.61 = (f32[128]{0:T(128)}, f32[128]{0:T(128)S(1)}, u32[]{:S(2)}) copy-start(f32[128]{0:T(128)S(1)} %multiply_power_fusion) | copy-start | bytes 1540
  156.2 42.4 %copy-start.47 = (f32[128]{0:T(128)}, f32[128]{0:T(128)S(1)}, u32[]{:S(2)}) copy-start(f32[128]{0:T(128)S(1)} %get-tuple-element.105) | copy-start | bytes 1540
  156.6 39.3 %copy-start.22 = (f32[128,256]{1,0:T(8,128)}, f32[128,256]{1,0:T(8,128)S(1)}, u32[]{:S(2)}) copy-start(f32[128,256]{1,0:T(8,128)S(1)} %get-tuple-element.115) | copy-start | bytes 393220
  158.2 46.1 %copy-start.26 = (f32[128,128]{1,0:T(8,128)}, f32[128,128]{1,0:T(8,128)S(1)}, u32[]{:S(2)}) copy-start(f32[128,128]{1,0:T(8,128)S(1)} %get-tuple-element.101) | copy-start | bytes 196612
  206.8 68.5 %copy-start.15 = (bf16[128,4,256]{0,2,1:T(8,128)(2,1)}, bf16[128,4,256]{0,2,1:T(8,128)(2,1)S(1)}, u32[]{:S(2)}) copy-start(bf16[128,4,256]{0,2,1:T(8,128)(2,1)S(1)} %fusion.23) | copy-start | bytes 786436
  210.9 64.5 %copy-start.57 = (f32[128]{0:T(128)}, f32[128]{0:T(128)S(1)}, u32[]{:S(2)}) copy-start(f32[128]{0:T(128)S(1)} %get-tuple-element.111) | copy-start | bytes 1540
  552.8 25.2 %copy-start.31 = (bf16[1024,256]{1,0:T(8,128)(2,1)S(1)}, bf16[1024,256]{1,0:T(8,128)(2,1)}, u32[]{:S(2)}) copy-start(bf16[1024,256]{1,0:T(8,128)(2,1)} %fusion.21) | copy-start | bytes 1572868
  552.8 25.2 %copy-start.32 = (bf16[1024,256]{1,0:T(8,128)(2,1)S(1)}, bf16[1024,256]{1,0:T(8,128)(2,1)}, u32[]{:S(2)}) copy-start(bf16[1024,256]{1,0:T(8,128)(2,1)} %fusion.20) | copy-start | bytes 1572868
  579.1 1587.4 %all-reduce.19.cloned.1.call-start = ((), (), s32[]{:S(2)}) async-start(), calls=%async_computation.7 | async-start | bytes 214695936
  580.9 30.1 %copy-start.60 = (f32[128]{0:T(128)S(1)}, f32[128]{0:T(128)}, u32[]{:S(2)}) copy-start(f32[128]{0:T(128)} %copy-done.59) | copy-start | bytes 1540
  580.9 30.1 %copy-start.62 = (f32[128]{0:T(128)S(1)}, f32[128]{0:T(128)}, u32[]{:S(2)}) copy-start(f32[128]{0:T(128)} %copy-done.61) | copy-start | bytes 1540
  580.9 30.4 %copy-start.23 = (f32[128,256]{1,0:T(8,128)S(1)}, f32[128,256]{1,0:T(8,128)}, u32[]{:S(2)}) copy-start(f32[128,256]{1,0:T(8,128)} %copy-done.22) | copy-start | bytes 393220
  581.0 30.4 %copy-start.50 = (f32[256]{0:T(256)S(1)}, f32[256]{0:T(256)}, u32[]{:S(2)}) copy-start(f32[256]{0:T(256)} %copy-done.49) | copy-start | bytes 3076
  581.0 30.4 %copy-start.56 = (f32[128]{0:T(128)S(1)}, f32[128]{0:T(128)}, u32[]{:S(2)}) copy-start(f32[128]{0:T(128)} %copy-done.55) | copy-start | bytes 1540
  581.0 30.6 %copy-start.65 = (f32[128]{0:T(128)S(1)}, f32[128]{0:T(128)}, u32[]{:S(2)}) copy-start(f32[128]{0:T(128)} %get-tuple-element.106) | copy-start | bytes 1540
  581.0 31.6 %copy-start.48 = (f32[128]{0:T(128)S(1)}, f32[128]{0:T(128)}, u32[]{:S(2)}) copy-start(f32[128]{0:T(128)} %copy-done.47) | copy-start | bytes 1540
  665.5 47.8 %copy-start.68 = (f32[128]{0:T(128)S(1)}, f32[128]{0:T(128)}, u32[]{:S(2)}) copy-start(f32[128]{0:T(128)} %get-tuple-element.104) | copy-start | bytes 1540
  666.4 46.9 %copy-start.11 = (f32[128,1152]{1,0:T(8,128)S(1)}, f32[128,1152]{1,0:T(8,128)}, u32[]{:S(2)}) copy-start(f32[128,1152]{1,0:T(8,128)} %copy-done.10) | copy-start | bytes 1769476
  (46 other events, 237.4 us)
Sparse Core Ops, SparseCore 0:
  10.9 60.5 all-gather.15
  74.5 56.8 all-gather.11
  134.4 122.4 all-gather.17
  259.7 116.8 all-gather.19
  379.3 108.8 all-gather.13
  579.2 30.8 reduce-scatter.1
  664.0 1502.4 all-reduce.18
where the time goes:
time: 2190 us; the launch traced here: 2180 us
  waiting for transfers between devices  1680 us (77%)
  blocking collectives  214 us (10%)
  matrix products  111 us (5%)
  other arithmetic  88 us (4%)
  local copies, waits for them, and re-layouts  72.5 us (3%)
    unnamed x8, waiting for transfers between devices  1460 us
    all_gather x1, waiting for transfers between devices, per_device(): lax.all_gather(up_weight, ('seq', 'ctx'), axis=0, tiled=True)  101 us
    unnamed x2, blocking collectives  82.6 us
    all_gather x1, waiting for transfers between devices, per_device(): lax.all_gather(down_weight, ('seq', 'ctx'), axis=0, tiled=True)  76.7 us
    unnamed x171, local copies, waits for them, and re-layouts  58.2 us
    concatenate x1, other arithmetic, per_device(): jnp.concatenate([transposed_times(normed, attention_backs), transposed_ti...  47.3 us
    all_gather x1, waiting for transfers between devices, per_device(): lax.all_gather(gate_weight, ('seq', 'ctx'), axis=0, tiled=True)  45.9 us
  transfers between devices with their start and end apart: 7, of which 5 were waited for; matrix products, arithmetic and copies ran while one was open for 5% of the time, Pallas kernels for 0%

commit v1 on v0

--- a/solution.py
+++ b/solution.py
@@ -3,6 +3,7 @@
 import jax.numpy as jnp
 from jax import lax
 from jax.sharding import PartitionSpec as P
+from jax.lax import all_to_all, axis_size
 
 D = 1152
 H = 4
@@ -137,7 +138,15 @@
     feedfwd_set = (
         lax.all_gather(feedfwd_gain, ("seq", "ctx"), axis=0, tiled=True),
         lax.all_gather(gate_weight, ("seq", "ctx"), axis=0, tiled=True),
-        lax.all_gather(up_weight, ("seq", "ctx"), axis=0, tiled=True),
+        jnp.concatenate(
+            all_to_all(
+                jnp.stack([up_weight for _ in range(axis_size(("seq", "ctx")))]),
+                ("seq", "ctx"),
+                0,
+                0,
+            ),
+            axis=0,
+        ),
         lax.all_gather(down_weight, ("seq", "ctx"), axis=0, tiled=True),
         lax.all_gather(feedfwd_post, ("seq", "ctx"), axis=0, tiled=True),
     )

time: 2190 us -> 2530 us (1.16)
  blocking collectives: 214 us -> 739 us
  waiting for transfers between devices: 1680 us -> 1460 us
    unnamed x2, blocking collectives: 82.6 us -> 603 us
    all_gather x1, waiting for transfers between devices: 101 us -> 0.01 us  [per_device(): lax.all_gather(up_weight, ('seq', 'ctx'), axis=0, tiled=True)]
    all_gather x1, waiting for transfers between devices: 76.7 us -> 0.01 us  [per_device(): lax.all_gather(down_weight, ('seq', 'ctx'), axis=0, tiled=True)]
    all_gather x1, waiting for transfers between devices: 45.9 us -> 0.02 us  [per_device(): lax.all_gather(gate_weight, ('seq', 'ctx'), axis=0, tiled=True)]
    unnamed x171 -> x187, local copies, waits for them, and re-layouts: 58.2 us -> 55.2 us
  transfers between devices with their start and end apart: 7 -> 8, of which waited for: 5 -> 2; matrix products, arithmetic and copies ran while one was open for 5% -> 6% of each run, Pallas kernels for 0% -> 0%
where the time goes in v1:
time: 2530 us; the launch traced here: 2520 us
  waiting for transfers between devices  1460 us (58%)
  blocking collectives  739 us (29%)
  matrix products  111 us (4%)
  local copies, waits for them, and re-layouts  95.5 us (4%)
  other arithmetic  87.3 us (3%)
    unnamed x8, waiting for transfers between devices  1460 us
    unnamed x2, blocking collectives  603 us
    unnamed x187, local copies, waits for them, and re-layouts  55.2 us
  transfers between devices with their start and end apart: 8, of which 2 were waited for; matrix products, arithmetic and copies ran while one was open for 6% of the time, Pallas kernels for 0%

profile of v1, /device:TPU:0, one launch (start us, length us, event | category | flops | bytes accessed | tf_op | source)
XLA Modules:
  0.0 2516.3 jit_solution(17446173298165265769)
XLA Ops:
  10.0 7.1 stack.2
  17.2 7.4 all-to-all-start
  26.8 562.6 %all-reduce.16 = (bf16[1152]{0:T(1024)(128)(2,1)S(1)}, bf16[256]{0:T(256)(128)(2,1)S(1)}, bf16[256]{0:T(256)(128)(2,1)S(1)}, bf16[1152]{0:T(1024)(128)(2,1)S(1)}...) all-reduce(bf16[1152]{0:T(1024)(128)(2,1)S(1)} %dynamic-update-slic, ...), channel_id=1, replica_groups=mesh['seq'=4,'ctx'=8] {'seq','ctx'}, use_global_device_ids=true, to_apply=%add | all-reduce | flops 5120 | bytes 20480
  591.2 46.3 %all-gather.2 = bf16[32,36,256]{2,1,0:T(8,128)(2,1)S(1)} all-gather(bf16[1,36,256]{2,1,0:T(8,128)(2,1)S(1)} %bitcast.148), channel_id=1, replica_groups=mesh['seq'=4,'ctx'=8] {'seq','ctx'}, dimensions={0}, use_global_device_ids=true | all-gather | bytes 608256 | tf_op jit(solution)/shard_map/all_gather | solution.py:131
  637.7 44.5 %all-gather = bf16[32,36,256]{2,1,0:T(8,128)(2,1)S(1)} all-gather(bf16[1,36,256]{2,1,0:T(8,128)(2,1)S(1)} %bitcast.149), channel_id=1, replica_groups=mesh['seq'=4,'ctx'=8] {'seq','ctx'}, dimensions={0}, use_global_device_ids=true | all-gather | bytes 608256 | tf_op jit(solution)/shard_map/all_gather | solution.py:132
  682.4 9.7 all-gather.1
  695.5 17.8 all_gather.63
  713.6 17.5 all_gather.59
  731.1 2.7 reshape.310
  741.9 2.4 multiply_reduce_fusion.6
  746.0 18.4 reshape.312
  764.5 18.8 reshape.288
  783.3 8.1 fusion.98
  791.5 1.8 copy-done.3
  794.6 4.7 multiply_convert_fusion.1
  799.3 8.2 multiply_reduce_fusion.4
  809.3 10.4 multiply_convert_fusion
  821.0 11.4 fusion.99
  832.3 18.4 reshape.314
  850.8 12.7 multiply_reduce_fusion
  863.5 2.3 multiply_reduce_fusion.1
  871.1 12.6 fusion.101
  883.6 25.1 fusion.7
  911.8 25.0 pad_maximum_fusion.1
  936.8 5.0 reduce-scatter.2.cloned.1.call-done
  944.2 4.0 fusion.57
  948.2 47.2 %pad_maximum_fusion = f32[1152,15360]{1,0:T(8,128)} fusion(f32[1152,13824]{1,0:T(8,128)} %fusion.7, f32[1152,1536]{1,0:T(8,128)} %fusion.57), kind=kLoop, calls=%fused_computation | loop fusion | flops 17694720 | bytes 141557760 | tf_op jit(solution)/shard_map/concatenate | solution.py:315
  1001.2 40.3 %all-reduce.14 = (f32[1152]{0:T(1024)S(1)}, f32[256]{0:T(256)S(1)}, f32[256]{0:T(256)S(1)}, f32[1152]{0:T(1024)S(1)}, f32[1152]{0:T(1024)S(1)}, /*index=5*/f32[1152]{0:T(1024)S(1)}) all-reduce(f32[1152]{0:T(1024)S(1)} %get-tuple-element.57, f32[256]{0:T(256)S(1)} %reduce_sum.205, ...), channel_id=3, replica_groups=mesh['seq'=4,'ctx'=8] {'seq','ctx'}, use_global_device_ids=true, to_apply=%region_16.17.clone | all-reduce | flops 5120 | bytes 40960
  1046.2 1452.2 %all-reduce.19.cloned.1.call-done = (f32[1152,15360]{1,0:T(8,128)}, f32[7936,1152]{1,0:T(8,128)}) async-done(((f32[1152,15360]{1,0:T(8,128)}, f32[7936,1152]{1,0:T(8,128)}), (f32[1152,15360]{1,0:T(8,128)}, f32[7936,1152]{1,0:T(8,128)})) %all-reduce.19.cloned.1.call-update) | async-done | bytes 107347984
  2499.9 2.2 constant_dynamic-slice_fusion.2
  2503.8 1.7 fusion.97
  2505.5 3.7 fusion.96
  (273 shorter events, 48.7 us)
Async XLA Ops:
  7.2 723.9 %all-gather.16.cloned.1.call-start = ((), (), s32[]{:S(2)}) async-start(), calls=%async_computation.5 | async-start | bytes 2703360 | tf_op jit(solution)/shard_map/all_gather | solution.py:130
  7.9 734.0 %all-gather.12.cloned.1.call-start = ((), (), s32[]{:S(2)}) async-start(), calls=%async_computation.2 | async-start | bytes 2433024 | tf_op jit(solution)/shard_map/all_gather | solution.py:135
  8.7 737.4 %all-gather.18.cloned.1.call-start = ((), (), s32[]{:S(2)}) async-start(), calls=%async_computation.6 | async-start | bytes 18247680 | tf_op jit(solution)/shard_map/all_gather | solution.py:140
  9.4 789.9 %all-gather.14.cloned.1.call-start = ((), (), s32[]{:S(2)}) async-start(), calls=%async_computation.3 | async-start | bytes 16422912 | tf_op jit(solution)/shard_map/all_gather | solution.py:150
  17.2 574.1 %copy-start.46 = (bf16[36,256]{1,0:T(8,128)(2,1)S(1)}, bf16[36,256]{1,0:T(8,128)(2,1)}, u32[]{:S(2)}) copy-start(bf16[36,256]{1,0:T(8,128)(2,1)} %param.20) | copy-start | bytes 55300
  17.2 620.5 %copy-start.47 = (bf16[36,256]{1,0:T(8,128)(2,1)S(1)}, bf16[36,256]{1,0:T(8,128)(2,1)}, u32[]{:S(2)}) copy-start(bf16[36,256]{1,0:T(8,128)(2,1)} %param.21) | copy-start | bytes 55300
  17.2 747.3 %all-to-all-start = ((bf16[32,36,6912]{2,1,0:T(8,128)(2,1)}), bf16[32,36,6912]{2,1,0:T(8,128)(2,1)}, u32[]{:S(2)}, u32[]{:S(2)}) async-start(bf16[32,36,6912]{2,1,0:T(8,128)(2,1)} %stack.2), calls=%async_computation | async-start | bytes 35389440 | tf_op jit(solution)/shard_map/all_to_all | solution.py:142
  24.6 667.4 %copy-start.5 = (bf16[128,1152]{1,0:T(8,128)(2,1)S(1)}, bf16[128,1152]{1,0:T(8,128)(2,1)}, u32[]{:S(2)}) copy-start(bf16[128,1152]{1,0:T(8,128)(2,1)} %param.16) | copy-start | bytes 884740
  24.6 807.7 %all-gather.20.cloned.1.call-start = ((), (), s32[]{:S(2)}) async-start(), calls=%async_computation.7 | async-start | bytes 18247680 | tf_op jit(solution)/shard_map/all_gather | solution.py:209
  25.2 916.6 %reduce-scatter.2.cloned.1.call-start = ((), (), s32[]{:S(2)}) async-start(), calls=%async_computation.4 | async-start | bytes 1179648 | tf_op jit(solution)/shard_map/reduce_scatter | solution.py:286
  25.3 688.2 %copy-start.61 = (f32[128]{0:T(128)}, f32[128]{0:T(128)S(1)}, u32[]{:S(2)}) copy-start(f32[128]{0:T(128)S(1)} %convert_element_type.95) | copy-start | bytes 1540
  589.4 104.3 %copy-start.51 = (f32[256]{0:T(256)}, f32[256]{0:T(256)S(1)}, u32[]{:S(2)}) copy-start(f32[256]{0:T(256)S(1)} %convert_element_type.94) | copy-start | bytes 3076
  589.4 149.8 %copy-start.53 = (f32[256]{0:T(256)}, f32[256]{0:T(256)S(1)}, u32[]{:S(2)}) copy-start(f32[256]{0:T(256)S(1)} %convert_element_type.96) | copy-start | bytes 3076
  637.7 93.3 %copy-start.14 = (bf16[1152,256]{1,0:T(8,128)(2,1)}, bf16[1152,256]{1,0:T(8,128)(2,1)S(1)}, u32[]{:S(2)}) copy-start(bf16[1152,256]{1,0:T(8,128)(2,1)S(1)} %reshape.308) | copy-start | bytes 1769476
  682.4 48.7 %copy-start.15 = (bf16[1152,256]{1,0:T(8,128)(2,1)}, bf16[1152,256]{1,0:T(8,128)(2,1)S(1)}, u32[]{:S(2)}) copy-start(bf16[1152,256]{1,0:T(8,128)(2,1)S(1)} %reshape.304) | copy-start | bytes 1769476
  692.1 41.7 %copy-start.63 = (f32[128]{0:T(128)}, f32[128]{0:T(128)S(1)}, u32[]{:S(2)}) copy-start(f32[128]{0:T(128)S(1)} %multiply_power_fusion) | copy-start | bytes 1540
  692.8 41.0 %copy-start.49 = (f32[128]{0:T(128)}, f32[128]{0:T(128)S(1)}, u32[]{:S(2)}) copy-start(f32[128]{0:T(128)S(1)} %get-tuple-element.105) | copy-start | bytes 1540
  693.1 37.9 %copy-start.23 = (f32[128,256]{1,0:T(8,128)}, f32[128,256]{1,0:T(8,128)S(1)}, u32[]{:S(2)}) copy-start(f32[128,256]{1,0:T(8,128)S(1)} %get-tuple-element.115) | copy-start | bytes 393220
  694.6 44.7 %copy-start.27 = (f32[128,128]{1,0:T(8,128)}, f32[128,128]{1,0:T(8,128)S(1)}, u32[]{:S(2)}) copy-start(f32[128,128]{1,0:T(8,128)S(1)} %get-tuple-element.101) | copy-start | bytes 196612
  883.6 25.1 copy-start.28
  883.6 25.2 copy-start.32
  883.6 25.2 %copy-start.33 = (bf16[1024,256]{1,0:T(8,128)(2,1)S(1)}, bf16[1024,256]{1,0:T(8,128)(2,1)}, u32[]{:S(2)}) copy-start(bf16[1024,256]{1,0:T(8,128)(2,1)} %fusion.20) | copy-start | bytes 1572868
  909.9 1588.4 %all-reduce.19.cloned.1.call-start = ((), (), s32[]{:S(2)}) async-start(), calls=%async_computation.8 | async-start | bytes 214695936
  911.7 31.0 %copy-start.62 = (f32[128]{0:T(128)S(1)}, f32[128]{0:T(128)}, u32[]{:S(2)}) copy-start(f32[128]{0:T(128)} %copy-done.61) | copy-start | bytes 1540
  911.8 31.0 %copy-start.64 = (f32[128]{0:T(128)S(1)}, f32[128]{0:T(128)}, u32[]{:S(2)}) copy-start(f32[128]{0:T(128)} %copy-done.63) | copy-start | bytes 1540
  911.8 31.3 %copy-start.24 = (f32[128,256]{1,0:T(8,128)S(1)}, f32[128,256]{1,0:T(8,128)}, u32[]{:S(2)}) copy-start(f32[128,256]{1,0:T(8,128)} %copy-done.23) | copy-start | bytes 393220
  911.8 31.3 %copy-start.52 = (f32[256]{0:T(256)S(1)}, f32[256]{0:T(256)}, u32[]{:S(2)}) copy-start(f32[256]{0:T(256)} %copy-done.51) | copy-start | bytes 3076
  911.8 31.3 %copy-start.58 = (f32[128]{0:T(128)S(1)}, f32[128]{0:T(128)}, u32[]{:S(2)}) copy-start(f32[128]{0:T(128)} %copy-done.57) | copy-start | bytes 1540
  911.8 31.5 %copy-start.67 = (f32[128]{0:T(128)S(1)}, f32[128]{0:T(128)}, u32[]{:S(2)}) copy-start(f32[128]{0:T(128)} %get-tuple-element.106) | copy-start | bytes 1540
  911.8 32.4 %copy-start.50 = (f32[128]{0:T(128)S(1)}, f32[128]{0:T(128)}, u32[]{:S(2)}) copy-start(f32[128]{0:T(128)} %copy-done.49) | copy-start | bytes 1540
  997.2 47.9 %copy-start.70 = (f32[128]{0:T(128)S(1)}, f32[128]{0:T(128)}, u32[]{:S(2)}) copy-start(f32[128]{0:T(128)} %get-tuple-element.104) | copy-start | bytes 1540
  998.0 47.0 %copy-start.11 = (f32[128,1152]{1,0:T(8,128)S(1)}, f32[128,1152]{1,0:T(8,128)}, u32[]{:S(2)}) copy-start(f32[128,1152]{1,0:T(8,128)} %copy-done.10) | copy-start | bytes 1769476
  (55 other events, 320.6 us)
Sparse Core Ops, SparseCore 0:
  10.8 129.4 all-gather.15
  143.3 126.4 all-gather.11
  272.8 187.4 all-gather.17
  463.0 128.8 all-gather.13
  594.8 128.8 all-gather.19
  910.0 31.7 reduce-scatter.1
  995.6 1502.6 all-reduce.18
